TPU v7x, 128 devices: a whole 4x4x4 slice. The times are simulated.
128 devices in a mesh: tm: 8 (over z, core), space: 16 (over y, x).
Axes of the slice: x: 4, y: 4, z: 4, core: 2. Of those that a mesh axis runs over, the one named last changes fastest.
Arguments:
- noise: bfloat16 [32, 1024, 8192], P('tm', 'space'), may hold values from -4 to 4
- scale: float32 [32, 8192], P('tm'), may hold values from 0.55 to 1
- tiles: bfloat16 [32, 64, 3, 128, 128], P('tm', 'space'), may hold values from -0.375 to 0.375
- columns: int32 [32, 64, 3], P('tm', 'space'), may hold values from 0 to 63, as said below
Outputs:
- samples: bfloat16 [32, 1024, 8192], P('tm', 'space')
Inputs may be any that keep to these rules, and one draw needn't show every extreme that they name: `columns`: in every tile row r of a time step the 3 entries are different, and the first is r itself.
All inputs are finite; a program needn't handle non-finite values.
Results may differ from a plain program's by a relative error of at most 0.03.
Values may be sent and summed in bfloat16 or wider, within the bound.
No kernel may reach another device: no remote copies, remote signals or barrier semaphores. Data moves between devices by JAX's collectives and lax.ppermute only.
A program may use at most 128 MiB of HBM per device.

v0:
```python
import jax
import jax.numpy as jnp
from jax import lax
from jax.sharding import PartitionSpec as P


def shifted(shard, axis, by):
    devices = lax.axis_size(axis)
    pairs = [(i, i + by) for i in range(devices) if 0 <= i + by < devices]
    return lax.ppermute(shard, axis, pairs)


def on_device(noise, scale, tiles, columns):
    step_count = noise.shape[0]
    local_samples = noise.shape[1]
    node_count = noise.shape[2]
    tile_count = tiles.shape[2]
    tile_size = tiles.shape[3]
    tile_rows = node_count // tile_size
    part_count = lax.axis_size("tm")
    my_part = lax.axis_index("tm")
    block_count = 1
    block_width = local_samples // block_count
    tiles_by_k = jnp.transpose(tiles, (0, 2, 1, 3, 4))
    columns_by_k = jnp.transpose(columns, (0, 2, 1))
    noise_rows = noise.reshape(step_count, local_samples, tile_rows, tile_size).transpose(
        0, 2, 1, 3
    )
    scale_rows = scale.reshape(step_count, tile_rows, 1, tile_size)
    full_tiles, full_columns = (
        lax.all_gather(tiles_by_k, "space", axis=2, tiled=True),
        lax.all_gather(columns_by_k, "space", axis=2, tiled=True),
    )

    def step_operands(time_step):
        return (full_tiles[time_step], full_columns[time_step])

    def sweep(incoming):
        current = incoming
        produced = [None] * step_count
        for reverse_step in range(step_count):
            time_step = step_count - 1 - reverse_step
            step_tile, step_column = step_operands(time_step)
            mixed = jnp.zeros((tile_rows, block_width, tile_size), jnp.float32)
            for which in range(tile_count):
                picked = jnp.take(current, step_column[which], axis=0)
                mixed = mixed + jnp.einsum(
                    "rsj,rij->rsi", picked, step_tile[which], preferred_element_type=jnp.float32
                )
            noise_block = noise_rows[time_step]
            updated = scale_rows[time_step] * (noise_block.astype(jnp.float32) + mixed)
            current = updated.astype(jnp.bfloat16)
            produced[time_step] = current
        return (current, jnp.stack(produced))

    def section(section_index, loop_carry):
        front, result = loop_carry
        incoming = shifted(front, "tm", -1)
        block_index = section_index - (part_count - 1 - my_part)
        active = (block_index >= 0) & (block_index < block_count)
        row_start = jnp.clip(block_index, 0, block_count - 1) * block_width
        first_field, block_out = sweep(incoming)
        chosen = jnp.where(active, block_out, result)
        new_result = lax.dynamic_update_slice_in_dim(result, chosen, row_start, 2)
        new_front = jnp.where(active, first_field, front)
        return (new_front, new_result)

    start_front = jnp.zeros((tile_rows, block_width, tile_size), jnp.bfloat16)
    start_result = jnp.zeros((step_count, tile_rows, local_samples, tile_size), jnp.bfloat16)
    _, result = lax.fori_loop(0, part_count + block_count - 1, section, (start_front, start_result))
    return result.transpose(0, 2, 1, 3).reshape(step_count, local_samples, node_count)


def solution(mesh):
    placed = (
        P("tm", "space", None),
        P("tm", None),
        P("tm", "space", None, None, None),
        P("tm", "space", None),
    )
    return jax.shard_map(
        on_device, mesh=mesh, in_specs=placed, out_specs=P("tm", "space", None), check_vma=False
    )
```

profile of v0, /device:TPU:0, one launch (start us, length us, event | category | flops | bytes accessed | tf_op | source)
XLA Modules:
  0.0 821.2 jit_solution(8011077418723320846)
XLA Ops:
  13.7 4.7 copy.14
  18.6 24.2 %all_gather.6 = s32[4,3,64]{1,0,2:T(4,128)S(1)} all-gather(s32[4,3,4]{1,0,2:T(4,128)S(1)} %bitcast.179), channel_id=1, replica_groups=mesh['tm'=8,'space'=16] {'space'}, dimensions={2}, use_global_device_ids=true | all-gather | bytes 3264 | tf_op jit(solution)/shard_map/all_gather | solution.py:32
  42.9 123.8 %all-gather.2.cloned.1.call-done = bf16[4,3,64,128,128]{4,3,2,1,0:T(8,128)(2,1)} async-done(((bf16[4,3,4,128,128]{4,3,2,1,0:T(8,128)(2,1)}), bf16[4,3,64,128,128]{4,3,2,1,0:T(8,128)(2,1)}) %all-gather.2.cloned.1.call-update) | async-done | bytes 25165840 | tf_op jit(solution)/shard_map/all_gather | solution.py:31
  166.7 642.8 %while.18 = (s32[]{:T(128)}, bf16[64,64,128]{2,1,0:T(8,128)(2,1)}, bf16[4,64,64,128]{3,2,1,0:T(8,128)(2,1)}, s32[]{:T(128)}, f32[4,64,1,128]{3,1,2,0:T(8,128)S(1...) while((s32[]{:T(128)}, bf16[64,64,128]{2,1,0:T(8,128)(2,1)}, ...), condition=%wide.region_1.0_spmd.clone, body=%wide.region_0.2_spmd.clone.sunk | while | flops 1641038336 | bytes 185005984 | solution.py:70
  178.2 4.8 fusion.158
  184.6 4.3 fusion.160
  228.1 4.6 broadcast_select_fusion.5
  238.7 14.1 %collective-permute-done = bf16[64,64,128]{2,1,0:T(8,128)(2,1)S(1)} collective-permute-done((bf16[64,64,128]{2,1,0:T(8,128)(2,1)S(1)}, bf16[64,64,128]{2,1,0:T(8,128)(2,1)S(1)}, u32[]{:S(2)}, u32[]{:S(2)}) %collective-permute-start) | collective-permute-done | bytes 1048608 | tf_op jit(solution)/shard_map/while/body/eval_jaxpr/ppermute | solution.py:10
  259.6 4.8 fusion.158
  266.1 4.3 fusion.160
  309.6 4.6 broadcast_select_fusion.5
  320.1 14.7 %collective-permute-done = bf16[64,64,128]{2,1,0:T(8,128)(2,1)S(1)} collective-permute-done((bf16[64,64,128]{2,1,0:T(8,128)(2,1)S(1)}, bf16[64,64,128]{2,1,0:T(8,128)(2,1)S(1)}, u32[]{:S(2)}, u32[]{:S(2)}) %collective-permute-start) | collective-permute-done | bytes 1048608 | tf_op jit(solution)/shard_map/while/body/eval_jaxpr/ppermute | solution.py:10
  341.6 4.8 fusion.158
  391.6 4.6 broadcast_select_fusion.5
  402.1 14.7 %collective-permute-done = bf16[64,64,128]{2,1,0:T(8,128)(2,1)S(1)} collective-permute-done((bf16[64,64,128]{2,1,0:T(8,128)(2,1)S(1)}, bf16[64,64,128]{2,1,0:T(8,128)(2,1)S(1)}, u32[]{:S(2)}, u32[]{:S(2)}) %collective-permute-start) | collective-permute-done | bytes 1048608 | tf_op jit(solution)/shard_map/while/body/eval_jaxpr/ppermute | solution.py:10
  423.7 4.8 fusion.158
  473.6 4.6 broadcast_select_fusion.5
  484.2 14.7 %collective-permute-done = bf16[64,64,128]{2,1,0:T(8,128)(2,1)S(1)} collective-permute-done((bf16[64,64,128]{2,1,0:T(8,128)(2,1)S(1)}, bf16[64,64,128]{2,1,0:T(8,128)(2,1)S(1)}, u32[]{:S(2)}, u32[]{:S(2)}) %collective-permute-start) | collective-permute-done | bytes 1048608 | tf_op jit(solution)/shard_map/while/body/eval_jaxpr/ppermute | solution.py:10
  505.7 4.8 fusion.158
  512.1 4.3 fusion.160
  555.6 4.6 broadcast_select_fusion.5
  566.2 14.7 %collective-permute-done = bf16[64,64,128]{2,1,0:T(8,128)(2,1)S(1)} collective-permute-done((bf16[64,64,128]{2,1,0:T(8,128)(2,1)S(1)}, bf16[64,64,128]{2,1,0:T(8,128)(2,1)S(1)}, u32[]{:S(2)}, u32[]{:S(2)}) %collective-permute-start) | collective-permute-done | bytes 1048608 | tf_op jit(solution)/shard_map/while/body/eval_jaxpr/ppermute | solution.py:10
  587.7 4.8 fusion.158
  637.7 4.6 broadcast_select_fusion.5
  648.2 14.7 %collective-permute-done = bf16[64,64,128]{2,1,0:T(8,128)(2,1)S(1)} collective-permute-done((bf16[64,64,128]{2,1,0:T(8,128)(2,1)S(1)}, bf16[64,64,128]{2,1,0:T(8,128)(2,1)S(1)}, u32[]{:S(2)}, u32[]{:S(2)}) %collective-permute-start) | collective-permute-done | bytes 1048608 | tf_op jit(solution)/shard_map/while/body/eval_jaxpr/ppermute | solution.py:10
  669.7 4.8 fusion.158
  719.7 4.6 broadcast_select_fusion.5
  730.2 14.7 %collective-permute-done = bf16[64,64,128]{2,1,0:T(8,128)(2,1)S(1)} collective-permute-done((bf16[64,64,128]{2,1,0:T(8,128)(2,1)S(1)}, bf16[64,64,128]{2,1,0:T(8,128)(2,1)S(1)}, u32[]{:S(2)}, u32[]{:S(2)}) %collective-permute-start) | collective-permute-done | bytes 1048608 | tf_op jit(solution)/shard_map/while/body/eval_jaxpr/ppermute | solution.py:10
  751.7 4.8 fusion.158
  758.2 4.3 fusion.160
  801.7 4.6 broadcast_select_fusion.5
  809.5 4.9 copy_bitcast_fusion
  (403 shorter events, 453.3 us)
Async XLA Ops:
  6.5 160.1 %all-gather.2.cloned.1.call-start = ((), (), s32[]{:S(2)}) async-start(), calls=%async_computation | async-start | bytes 26738688 | tf_op jit(solution)/shard_map/all_gather | solution.py:31
  13.7 4.7 copy-start.9
  13.7 29.1 %copy-start.8 = (f32[4,8192]{1,0:T(4,128)S(1)}, f32[4,8192]{1,0:T(4,128)}, u32[]{:S(2)}) copy-start(f32[4,8192]{1,0:T(4,128)} %param.9) | copy-start | bytes 393220
  166.7 6.3 copy-start.2
  166.8 4.6 collective-permute-start
  221.2 3.5 copy-start.7
  228.1 4.6 copy-start
  237.2 17.3 %copy-start.2 = (bf16[64,64,128]{2,1,0:T(8,128)(2,1)}, bf16[64,64,128]{2,1,0:T(8,128)(2,1)S(1)}, u32[]{:S(2)}) copy-start(bf16[64,64,128]{2,1,0:T(8,128)(2,1)S(1)} %broadcast_select_fusion.4) | copy-start | bytes 3145732 | tf_op jit(solution)/shard_map/while
  237.2 15.5 %collective-permute-start = (bf16[64,64,128]{2,1,0:T(8,128)(2,1)S(1)}, bf16[64,64,128]{2,1,0:T(8,128)(2,1)S(1)}, u32[]{:S(2)}, u32[]{:S(2)}) collective-permute-start(bf16[64,64,128]{2,1,0:T(8,128)(2,1)S(1)} %broadcast_select_fusion.4), channel_id=1, source_target_pairs={{16,0},{32,16},{48,32},{64,48},{80,64},{96,80},{112,96},{17,1},{33... | collective-permute-start | bytes 3145736 | tf_op jit(solution)/shard_map/while/body/eval_jaxpr/ppermute | solution.py:10
  302.7 3.5 copy-start.7
  309.6 4.6 copy-start
  318.7 17.8 %copy-start.2 = (bf16[64,64,128]{2,1,0:T(8,128)(2,1)}, bf16[64,64,128]{2,1,0:T(8,128)(2,1)S(1)}, u32[]{:S(2)}) copy-start(bf16[64,64,128]{2,1,0:T(8,128)(2,1)S(1)} %broadcast_select_fusion.4) | copy-start | bytes 3145732 | tf_op jit(solution)/shard_map/while
  318.7 16.1 %collective-permute-start = (bf16[64,64,128]{2,1,0:T(8,128)(2,1)S(1)}, bf16[64,64,128]{2,1,0:T(8,128)(2,1)S(1)}, u32[]{:S(2)}, u32[]{:S(2)}) collective-permute-start(bf16[64,64,128]{2,1,0:T(8,128)(2,1)S(1)} %broadcast_select_fusion.4), channel_id=1, source_target_pairs={{16,0},{32,16},{48,32},{64,48},{80,64},{96,80},{112,96},{17,1},{33... | collective-permute-start | bytes 3145736 | tf_op jit(solution)/shard_map/while/body/eval_jaxpr/ppermute | solution.py:10
  384.7 3.5 copy-start.7
  391.6 4.6 copy-start
  400.7 17.8 %copy-start.2 = (bf16[64,64,128]{2,1,0:T(8,128)(2,1)}, bf16[64,64,128]{2,1,0:T(8,128)(2,1)S(1)}, u32[]{:S(2)}) copy-start(bf16[64,64,128]{2,1,0:T(8,128)(2,1)S(1)} %broadcast_select_fusion.4) | copy-start | bytes 3145732 | tf_op jit(solution)/shard_map/while
  400.7 16.1 %collective-permute-start = (bf16[64,64,128]{2,1,0:T(8,128)(2,1)S(1)}, bf16[64,64,128]{2,1,0:T(8,128)(2,1)S(1)}, u32[]{:S(2)}, u32[]{:S(2)}) collective-permute-start(bf16[64,64,128]{2,1,0:T(8,128)(2,1)S(1)} %broadcast_select_fusion.4), channel_id=1, source_target_pairs={{16,0},{32,16},{48,32},{64,48},{80,64},{96,80},{112,96},{17,1},{33... | collective-permute-start | bytes 3145736 | tf_op jit(solution)/shard_map/while/body/eval_jaxpr/ppermute | solution.py:10
  466.7 3.5 copy-start.7
  473.6 4.6 copy-start
  482.7 17.8 %copy-start.2 = (bf16[64,64,128]{2,1,0:T(8,128)(2,1)}, bf16[64,64,128]{2,1,0:T(8,128)(2,1)S(1)}, u32[]{:S(2)}) copy-start(bf16[64,64,128]{2,1,0:T(8,128)(2,1)S(1)} %broadcast_select_fusion.4) | copy-start | bytes 3145732 | tf_op jit(solution)/shard_map/while
  482.7 16.1 %collective-permute-start = (bf16[64,64,128]{2,1,0:T(8,128)(2,1)S(1)}, bf16[64,64,128]{2,1,0:T(8,128)(2,1)S(1)}, u32[]{:S(2)}, u32[]{:S(2)}) collective-permute-start(bf16[64,64,128]{2,1,0:T(8,128)(2,1)S(1)} %broadcast_select_fusion.4), channel_id=1, source_target_pairs={{16,0},{32,16},{48,32},{64,48},{80,64},{96,80},{112,96},{17,1},{33... | collective-permute-start | bytes 3145736 | tf_op jit(solution)/shard_map/while/body/eval_jaxpr/ppermute | solution.py:10
  548.8 3.5 copy-start.7
  555.6 4.6 copy-start
  564.7 17.8 %copy-start.2 = (bf16[64,64,128]{2,1,0:T(8,128)(2,1)}, bf16[64,64,128]{2,1,0:T(8,128)(2,1)S(1)}, u32[]{:S(2)}) copy-start(bf16[64,64,128]{2,1,0:T(8,128)(2,1)S(1)} %broadcast_select_fusion.4) | copy-start | bytes 3145732 | tf_op jit(solution)/shard_map/while
  564.7 16.1 %collective-permute-start = (bf16[64,64,128]{2,1,0:T(8,128)(2,1)S(1)}, bf16[64,64,128]{2,1,0:T(8,128)(2,1)S(1)}, u32[]{:S(2)}, u32[]{:S(2)}) collective-permute-start(bf16[64,64,128]{2,1,0:T(8,128)(2,1)S(1)} %broadcast_select_fusion.4), channel_id=1, source_target_pairs={{16,0},{32,16},{48,32},{64,48},{80,64},{96,80},{112,96},{17,1},{33... | collective-permute-start | bytes 3145736 | tf_op jit(solution)/shard_map/while/body/eval_jaxpr/ppermute | solution.py:10
  637.7 4.6 copy-start
  646.7 17.8 %copy-start.2 = (bf16[64,64,128]{2,1,0:T(8,128)(2,1)}, bf16[64,64,128]{2,1,0:T(8,128)(2,1)S(1)}, u32[]{:S(2)}) copy-start(bf16[64,64,128]{2,1,0:T(8,128)(2,1)S(1)} %broadcast_select_fusion.4) | copy-start | bytes 3145732 | tf_op jit(solution)/shard_map/while
  646.7 16.1 %collective-permute-start = (bf16[64,64,128]{2,1,0:T(8,128)(2,1)S(1)}, bf16[64,64,128]{2,1,0:T(8,128)(2,1)S(1)}, u32[]{:S(2)}, u32[]{:S(2)}) collective-permute-start(bf16[64,64,128]{2,1,0:T(8,128)(2,1)S(1)} %broadcast_select_fusion.4), channel_id=1, source_target_pairs={{16,0},{32,16},{48,32},{64,48},{80,64},{96,80},{112,96},{17,1},{33... | collective-permute-start | bytes 3145736 | tf_op jit(solution)/shard_map/while/body/eval_jaxpr/ppermute | solution.py:10
  719.7 4.6 copy-start
  728.8 17.8 %copy-start.2 = (bf16[64,64,128]{2,1,0:T(8,128)(2,1)}, bf16[64,64,128]{2,1,0:T(8,128)(2,1)S(1)}, u32[]{:S(2)}) copy-start(bf16[64,64,128]{2,1,0:T(8,128)(2,1)S(1)} %broadcast_select_fusion.4) | copy-start | bytes 3145732 | tf_op jit(solution)/shard_map/while
  728.8 16.1 %collective-permute-start = (bf16[64,64,128]{2,1,0:T(8,128)(2,1)S(1)}, bf16[64,64,128]{2,1,0:T(8,128)(2,1)S(1)}, u32[]{:S(2)}, u32[]{:S(2)}) collective-permute-start(bf16[64,64,128]{2,1,0:T(8,128)(2,1)S(1)} %broadcast_select_fusion.4), channel_id=1, source_target_pairs={{16,0},{32,16},{48,32},{64,48},{80,64},{96,80},{112,96},{17,1},{33... | collective-permute-start | bytes 3145736 | tf_op jit(solution)/shard_map/while/body/eval_jaxpr/ppermute | solution.py:10
  801.7 4.6 copy-start
  (43 other events, 130.9 us)
Sparse Core Ops, SparseCore 0:
  9.5 157.1 all-gather.1
where the time goes:
time: 836 us; the launch traced here: 821 us
  matrix products  350 us (42%)
  waiting for transfers between devices  229 us (27%)
  local copies, waits for them, and re-layouts  173 us (21%)
  blocking collectives  24.2 us (3%)
  other arithmetic  18.9 us (2%)
  between operations  13.5 us (2%)
  starting transfers between devices  10.3 us (1%)
    dot_general x96, matrix products, sweep(): jnp.einsum('rsj,rij->rsi', picked, step_tile[which], preferred_element_ty...  350 us
    gather x96, local copies, waits for them, and re-layouts, sweep(): picked = jnp.take(current, step_column[which], axis=0)  140 us
    all_gather x1, waiting for transfers between devices, on_device(): lax.all_gather(tiles_by_k, 'space', axis=2, tiled=True)  124 us
    ppermute x8, waiting for transfers between devices, shifted(): return lax.ppermute(shard, axis, pairs)  105 us
    all_gather x1, blocking collectives, on_device(): lax.all_gather(columns_by_k, 'space', axis=2, tiled=True)  24.2 us
  transfers between devices with their start and end apart: 9, of which 9 were waited for; matrix products, arithmetic and copies ran while one was open for 1% of the time, Pallas kernels for 0%

commit v1 on v0

v1 whole, which is shorter than its diff:
```python
import functools
import jax
import jax.numpy as jnp
from jax import lax
from jax.experimental import pallas as pl
from jax.experimental.pallas import tpu as pltpu
from jax.sharding import PartitionSpec as P

BLOCKS = 2
GROUP = 16


def sweep_kernel(
    steps, rows, width, group, block,
    state, columns, tiles, noise, scale, front, _, out, front_out,
    tile_buf, noise_buf, *rest,
):
    fields = rest[:steps]
    tile_sem, noise_sem, out_sem = rest[steps:]
    size = tiles.shape[-1]
    kt = tiles.shape[2] // size
    groups = rows // group
    mine = pl.ds(block * width, width)

    def tile_copy(s, g):
        part = pl.ds(g * group, group)
        return pltpu.make_async_copy(tiles.at[s, part], tile_buf.at[s, part], tile_sem.at[s, g])

    def noise_copy(s):
        return pltpu.make_async_copy(noise.at[s, mine], noise_buf.at[s], noise_sem.at[s])

    def out_copy(s):
        return pltpu.make_async_copy(fields[s], out.at[s, mine], out_sem.at[s])

    @pl.when(state[0] == 1)
    def _active():
        for s in reversed(range(steps)):
            noise_copy(s).start()
            for g in range(groups):
                tile_copy(s, g).start()
        for s in reversed(range(steps)):
            source = front if s == steps - 1 else fields[s + 1]
            target = fields[s]
            noise_copy(s).wait()

            def one_group(g, carry):
                tile_copy(s, g).wait()
                picked = []
                for q in range(group):
                    r = g * group + q
                    picked.append([
                        source[:, pl.ds(pl.multiple_of(columns[(s * rows + r) * kt + k] * size, size), size)]
                        for k in range(kt)
                    ])
                mixed = [
                    jnp.dot(
                        jnp.concatenate(picked[q], axis=1),
                        tile_buf[s, g * group + q],
                        preferred_element_type=jnp.float32,
                    )
                    for q in range(group)
                ]
                for q in range(group):
                    lanes = pl.ds(pl.multiple_of((g * group + q) * size, size), size)
                    total = noise_buf[s, :, lanes].astype(jnp.float32) + mixed[q]
                    value = (scale[s : s + 1, lanes] * total).astype(jnp.bfloat16)
                    target[:, lanes] = value
                    if s == 0:
                        front_out[:, lanes] = value
                return carry

            lax.fori_loop(0, groups, one_group, 0)
            out_copy(s).start()
        for s in range(steps):
            out_copy(s).wait()


def sweep(state, columns, tiles, noise, scale, front, out, block, width):
    steps, rows = tiles.shape[:2]
    node_count = noise.shape[-1]
    group = min(GROUP, rows)
    groups = rows // group
    anywhere = pl.BlockSpec(memory_space=pl.ANY)
    smem = pl.BlockSpec(memory_space=pltpu.SMEM)
    vmem = pl.BlockSpec(memory_space=pltpu.VMEM)
    return pl.pallas_call(
        functools.partial(sweep_kernel, steps, rows, width, group, block),
        out_shape=(
            jax.ShapeDtypeStruct(out.shape, out.dtype),
            jax.ShapeDtypeStruct(front.shape, front.dtype),
        ),
        in_specs=[smem, smem, anywhere, anywhere, vmem, vmem, anywhere],
        out_specs=(anywhere, vmem),
        input_output_aliases={6: 0},
        scratch_shapes=[
            pltpu.VMEM(tiles.shape, jnp.bfloat16),
            pltpu.VMEM((steps, width, node_count), jnp.bfloat16),
            *[pltpu.VMEM((width, node_count), jnp.bfloat16) for _ in range(steps)],
            pltpu.SemaphoreType.DMA((steps, groups)),
            pltpu.SemaphoreType.DMA((steps,)),
            pltpu.SemaphoreType.DMA((steps,)),
        ],
        compiler_params=pltpu.CompilerParams(vmem_limit_bytes=56 << 20),
        name="sweep",
    )(state, columns, tiles, noise, scale, front, out)


def on_device(noise, scale, tiles, columns):
    steps, local_samples, node_count = noise.shape
    local_rows, kt, size = tiles.shape[1:4]
    parts = lax.axis_size("tm")
    me = lax.axis_index("tm")
    width = local_samples // BLOCKS
    turned = jnp.swapaxes(tiles, 3, 4).reshape(steps, local_rows, kt * size, size)
    full_tiles = lax.all_gather(turned, "space", axis=1, tiled=True)
    full_columns = lax.all_gather(columns, "space", axis=1, tiled=True).reshape(-1)

    out = jnp.zeros(noise.shape, jnp.bfloat16)
    fronts = [jnp.zeros((width, node_count), jnp.bfloat16) for _ in range(BLOCKS)]
    for part in reversed(range(parts)):
        state = (me == part).astype(jnp.int32).reshape(1)
        for block in range(BLOCKS):
            out, front = sweep(
                state, full_columns, full_tiles, noise, scale, fronts[block], out, block, width
            )
            if part > 0:
                fronts[block] = lax.ppermute(front, "tm", [(part, part - 1)])
    return out


def solution(mesh):
    placed = (
        P("tm", "space", None),
        P("tm", None),
        P("tm", "space", None, None, None),
        P("tm", "space", None),
    )
    return jax.shard_map(
        on_device, mesh=mesh, in_specs=placed, out_specs=P("tm", "space", None), check_vma=False
    )
```

time: 836 us -> 371 us (0.44); the launches traced: 821 us -> 370 us
  matrix products: 350 us -> 0 us
  local copies, waits for them, and re-layouts: 173 us -> 18.1 us
  Pallas kernels: 0 us -> 62.6 us
  other arithmetic: 18.9 us -> 0 us
  waiting for transfers between devices: 229 us -> 241 us
    dot_general x96 -> x0, matrix products: 350 us -> none  [sweep(): jnp.einsum('rsj,rij->rsi', picked, step_tile[which], preferred_element_ty...]
    gather x96 -> x0, local copies, waits for them, and re-layouts: 140 us -> none  [sweep(): picked = jnp.take(current, step_column[which], axis=0)]
    pallas_call x0 -> x16, Pallas kernels: none -> 62.6 us  [sweep(): pl.pallas_call(functools.partial(sweep_kernel, steps, rows, width, group,...]
    while x128 -> x0, local copies, waits for them, and re-layouts: 16 us -> none
    select_n x8 -> x0, other arithmetic: 9.24 us -> none  [section(): chosen = jnp.where(active, block_out, result)]
    while x8 -> x0, other arithmetic: 9.15 us -> none
    ppermute x8 -> x14, waiting for transfers between devices: 105 us -> 109 us  [on_device(): fronts[block] = lax.ppermute(front, 'tm', [(part, part - 1)])]
  transfers between devices with their start and end apart: 9 -> 15, of which waited for: 9 -> 3; matrix products, arithmetic and copies ran while one was open for 1% -> 0% of each run, Pallas kernels for 0% -> 12%
where the time goes in v1:
time: 371 us; the launch traced here: 370 us
  waiting for transfers between devices  241 us (65%)
  Pallas kernels  62.6 us (17%)
  blocking collectives  24.2 us (7%)
  local copies, waits for them, and re-layouts  18.1 us (5%)
  between operations  13.9 us (4%)
  starting transfers between devices  10.9 us (3%)
    all_gather x1, waiting for transfers between devices, on_device(): full_tiles = lax.all_gather(turned, 'space', axis=1, tiled=True)  132 us
    ppermute x14, waiting for transfers between devices, on_device(): fronts[block] = lax.ppermute(front, 'tm', [(part, part - 1)])  109 us
    pallas_call x16, Pallas kernels, sweep(): pl.pallas_call(functools.partial(sweep_kernel, steps, rows, width, group,...  62.6 us
    all_gather x1, blocking collectives, on_device(): lax.all_gather(columns, 'space', axis=1, tiled=True).reshape(-1)  24.2 us
    unnamed x31, local copies, waits for them, and re-layouts  11.4 us
    ppermute x14, starting transfers between devices, on_device(): fronts[block] = lax.ppermute(front, 'tm', [(part, part - 1)])  10.9 us
  transfers between devices with their start and end apart: 15, of which 3 were waited for; matrix products, arithmetic and copies ran while one was open for 0% of the time, Pallas kernels for 12%

profile of v1, /device:TPU:0, one launch (start us, length us, event | category | flops | bytes accessed | tf_op | source)
XLA Modules:
  0.0 370.3 jit_solution(1792778208133052469)
XLA Ops:
  6.5 2.6 copy.26
  9.3 24.2 %all_gather.6 = s32[4,64,3]{2,0,1:T(4,128)S(1)} all-gather(s32[4,4,3]{2,0,1:T(4,128)S(1)} %copy.24), channel_id=1, replica_groups=mesh['tm'=8,'space'=16] {'space'}, dimensions={1}, use_global_device_ids=true | all-gather | bytes 3264 | tf_op jit(solution)/shard_map/all_gather | solution.py:116
  34.3 132.1 %all-gather.2.cloned.1.call-done.tiles = bf16[4,64,384,128]{3,2,1,0:T(8,128)(2,1)} async-done(((bf16[4,4,384,128]{3,2,1,0:T(8,128)(2,1)}), bf16[4,64,384,128]{3,2,1,0:T(8,128)(2,1)}) %all-gather.2.cloned.1.call-update) | async-done | bytes 25165840 | tf_op jit(solution)/shard_map/all_gather | solution.py:115
  166.3 0.8 broadcast_1_front.2.front
  167.2 2.5 broadcast_in_dim.3._
  169.6 2.1 sweep.16
  172.5 2.2 sweep.17
  175.4 0.8 copy-done.13
  176.2 2.1 sweep.18
  179.9 2.2 sweep.19
  182.8 0.8 copy-done.1
  183.6 2.1 sweep.20
  186.4 0.8 copy-done.7
  187.2 2.2 sweep.21
  190.1 0.8 copy-done.2
  190.9 2.3 sweep.22
  194.8 2.2 sweep.23
  197.7 0.8 copy-done.3
  198.5 2.1 sweep.24
  202.2 2.2 sweep.25
  205.1 0.8 copy-done.4
  205.9 2.1 sweep.26
  209.5 2.2 sweep.27
  213.2 2.1 sweep.28
  215.4 1.3 collective-permute-start.13
  217.5 2.4 sweep.29
  219.9 1.3 collective-permute-start.12
  221.2 106.9 %collective-permute-done.13.front = bf16[32,8192]{1,0:T(8,128)(2,1)S(1)} collective-permute-done((bf16[32,8192]{1,0:T(8,128)(2,1)}, bf16[32,8192]{1,0:T(8,128)(2,1)S(1)}, u32[]{:S(2)}, u32[]{:S(2)}) %collective-permute-start.13) | collective-permute-done | bytes 524320 | tf_op jit(solution)/shard_map/ppermute | solution.py:127
  328.9 16.1 %sweep.30 = (bf16[4,64,8192]{2,1,0:T(8,128)(2,1)}, bf16[32,8192]{1,0:T(8,128)(2,1)}) custom-call(s32[1]{0:T(128)} %bitcast.state, s32[768]{0:T(1024)} %reshape.48.columns, bf16[4,64,384,128]{3,2,1,0:T(8,128)(2,1)} %all-gather.2.cloned.1.call-done.tiles, bf16[4,64,8192]{2,1,0:T(8,128)(2,1)} %noise.31, ...), custom_call_target="tpu_custom_call", output_to_operand_aliasing={{0}: (6, {})} | custom-call | tf_op jit(solution)/shard_map/sweep/pallas_call | solution.py:86
  345.0 1.6 collective-permute-done.12.front
  346.6 0.8 copy-done.12
  347.4 16.0 %sweep.31 = (bf16[4,64,8192]{2,1,0:T(8,128)(2,1)}, bf16[32,8192]{1,0:T(8,128)(2,1)}) custom-call(s32[1]{0:T(128)} %bitcast.state, s32[768]{0:T(1024)} %reshape.48.columns, bf16[4,64,384,128]{3,2,1,0:T(8,128)(2,1)} %all-gather.2.cloned.1.call-done.tiles, bf16[4,64,8192]{2,1,0:T(8,128)(2,1)} %noise.31, ...), custom_call_target="tpu_custom_call", output_to_operand_aliasing={{0}: (6, {})} | custom-call | tf_op jit(solution)/shard_map/sweep/pallas_call | solution.py:86
  (52 shorter events, 14.9 us)
Async XLA Ops:
  6.5 2.6 copy-start.14
  6.5 159.8 %all-gather.2.cloned.1.call-start = ((), (), s32[]{:S(2)}) async-start(), calls=%async_computation | async-start | bytes 26738688 | tf_op jit(solution)/shard_map/all_gather | solution.py:115
  171.8 3.6 collective-permute-start.1
  174.7 4.4 %collective-permute-start = (bf16[32,8192]{1,0:T(8,128)(2,1)}, bf16[32,8192]{1,0:T(8,128)(2,1)S(1)}, u32[]{:S(2)}, u32[]{:S(2)}) collective-permute-start(bf16[32,8192]{1,0:T(8,128)(2,1)} %get-tuple-element.36), channel_id=1, source_target_pairs={{112,96},{113,97},{114,98},{115,99},{116,100},{117,101},{118,102},... | collective-permute-start | bytes 1572872 | tf_op jit(solution)/shard_map/ppermute | solution.py:127
  175.4 0.8 copy-start.13
  178.3 4.4 %collective-permute-start.3 = (bf16[32,8192]{1,0:T(8,128)(2,1)}, bf16[32,8192]{1,0:T(8,128)(2,1)S(1)}, u32[]{:S(2)}, u32[]{:S(2)}) collective-permute-start(bf16[32,8192]{1,0:T(8,128)(2,1)} %get-tuple-element.41), channel_id=1, source_target_pairs={{96,80},{97,81},{98,82},{99,83},{100,84},{101,85},{102,86},{103,87... | collective-permute-start | bytes 1572872 | tf_op jit(solution)/shard_map/ppermute | solution.py:127
  179.1 0.8 copy-start.6
  182.0 4.4 %collective-permute-start.2 = (bf16[32,8192]{1,0:T(8,128)(2,1)}, bf16[32,8192]{1,0:T(8,128)(2,1)S(1)}, u32[]{:S(2)}, u32[]{:S(2)}) collective-permute-start(bf16[32,8192]{1,0:T(8,128)(2,1)} %get-tuple-element.40), channel_id=1, source_target_pairs={{96,80},{97,81},{98,82},{99,83},{100,84},{101,85},{102,86},{103,87... | collective-permute-start | bytes 1572872 | tf_op jit(solution)/shard_map/ppermute | solution.py:127
  182.8 0.8 copy-start.1
  185.7 4.4 %collective-permute-start.5 = (bf16[32,8192]{1,0:T(8,128)(2,1)}, bf16[32,8192]{1,0:T(8,128)(2,1)S(1)}, u32[]{:S(2)}, u32[]{:S(2)}) collective-permute-start(bf16[32,8192]{1,0:T(8,128)(2,1)} %get-tuple-element.45), channel_id=1, source_target_pairs={{80,64},{81,65},{82,66},{83,67},{84,68},{85,69},{86,70},{87,71},{8... | collective-permute-start | bytes 1572872 | tf_op jit(solution)/shard_map/ppermute | solution.py:127
  186.4 0.8 copy-start.7
  189.4 4.6 %collective-permute-start.4 = (bf16[32,8192]{1,0:T(8,128)(2,1)}, bf16[32,8192]{1,0:T(8,128)(2,1)S(1)}, u32[]{:S(2)}, u32[]{:S(2)}) collective-permute-start(bf16[32,8192]{1,0:T(8,128)(2,1)} %get-tuple-element.44), channel_id=1, source_target_pairs={{80,64},{81,65},{82,66},{83,67},{84,68},{85,69},{86,70},{87,71},{8... | collective-permute-start | bytes 1572872 | tf_op jit(solution)/shard_map/ppermute | solution.py:127
  190.1 0.8 copy-start.2
  193.3 4.4 %collective-permute-start.7 = (bf16[32,8192]{1,0:T(8,128)(2,1)}, bf16[32,8192]{1,0:T(8,128)(2,1)S(1)}, u32[]{:S(2)}, u32[]{:S(2)}) collective-permute-start(bf16[32,8192]{1,0:T(8,128)(2,1)} %get-tuple-element.49), channel_id=1, source_target_pairs={{64,48},{65,49},{66,50},{67,51},{68,52},{69,53},{70,54},{71,55},{7... | collective-permute-start | bytes 1572872 | tf_op jit(solution)/shard_map/ppermute | solution.py:127
  194.0 0.8 copy-start.8
  197.0 4.4 %collective-permute-start.6 = (bf16[32,8192]{1,0:T(8,128)(2,1)}, bf16[32,8192]{1,0:T(8,128)(2,1)S(1)}, u32[]{:S(2)}, u32[]{:S(2)}) collective-permute-start(bf16[32,8192]{1,0:T(8,128)(2,1)} %get-tuple-element.48), channel_id=1, source_target_pairs={{64,48},{65,49},{66,50},{67,51},{68,52},{69,53},{70,54},{71,55},{7... | collective-permute-start | bytes 1572872 | tf_op jit(solution)/shard_map/ppermute | solution.py:127
  197.7 0.8 copy-start.3
  200.6 4.4 %collective-permute-start.9 = (bf16[32,8192]{1,0:T(8,128)(2,1)}, bf16[32,8192]{1,0:T(8,128)(2,1)S(1)}, u32[]{:S(2)}, u32[]{:S(2)}) collective-permute-start(bf16[32,8192]{1,0:T(8,128)(2,1)} %get-tuple-element.53), channel_id=1, source_target_pairs={{48,32},{49,33},{50,34},{51,35},{52,36},{53,37},{54,38},{55,39},{5... | collective-permute-start | bytes 1572872 | tf_op jit(solution)/shard_map/ppermute | solution.py:127
  201.4 0.8 copy-start.9
  204.3 4.4 %collective-permute-start.8 = (bf16[32,8192]{1,0:T(8,128)(2,1)}, bf16[32,8192]{1,0:T(8,128)(2,1)S(1)}, u32[]{:S(2)}, u32[]{:S(2)}) collective-permute-start(bf16[32,8192]{1,0:T(8,128)(2,1)} %get-tuple-element.52), channel_id=1, source_target_pairs={{48,32},{49,33},{50,34},{51,35},{52,36},{53,37},{54,38},{55,39},{5... | collective-permute-start | bytes 1572872 | tf_op jit(solution)/shard_map/ppermute | solution.py:127
  205.1 0.8 copy-start.4
  208.0 4.4 %collective-permute-start.11 = (bf16[32,8192]{1,0:T(8,128)(2,1)}, bf16[32,8192]{1,0:T(8,128)(2,1)S(1)}, u32[]{:S(2)}, u32[]{:S(2)}) collective-permute-start(bf16[32,8192]{1,0:T(8,128)(2,1)} %get-tuple-element.57), channel_id=1, source_target_pairs={{32,16},{33,17},{34,18},{35,19},{36,20},{37,21},{38,22},{39,23},{4... | collective-permute-start | bytes 1572872 | tf_op jit(solution)/shard_map/ppermute | solution.py:127
  208.7 0.8 copy-start.10
  211.7 5.0 %collective-permute-start.10 = (bf16[32,8192]{1,0:T(8,128)(2,1)}, bf16[32,8192]{1,0:T(8,128)(2,1)S(1)}, u32[]{:S(2)}, u32[]{:S(2)}) collective-permute-start(bf16[32,8192]{1,0:T(8,128)(2,1)} %get-tuple-element.56), channel_id=1, source_target_pairs={{32,16},{33,17},{34,18},{35,19},{36,20},{37,21},{38,22},{39,23},{4... | collective-permute-start | bytes 1572872 | tf_op jit(solution)/shard_map/ppermute | solution.py:127
  212.4 0.8 copy-start.5
  215.4 112.7 %collective-permute-start.13 = (bf16[32,8192]{1,0:T(8,128)(2,1)}, bf16[32,8192]{1,0:T(8,128)(2,1)S(1)}, u32[]{:S(2)}, u32[]{:S(2)}) collective-permute-start(bf16[32,8192]{1,0:T(8,128)(2,1)} %get-tuple-element.61), channel_id=1, source_target_pairs={{16,0},{17,1},{18,2},{19,3},{20,4},{21,5},{22,6},{23,7},{24,8},{25... | collective-permute-start | bytes 1572872 | tf_op jit(solution)/shard_map/ppermute | solution.py:127
  216.7 0.8 copy-start.11
  219.9 126.7 %collective-permute-start.12 = (bf16[32,8192]{1,0:T(8,128)(2,1)}, bf16[32,8192]{1,0:T(8,128)(2,1)S(1)}, u32[]{:S(2)}, u32[]{:S(2)}) collective-permute-start(bf16[32,8192]{1,0:T(8,128)(2,1)} %get-tuple-element.60), channel_id=1, source_target_pairs={{16,0},{17,1},{18,2},{19,3},{20,4},{21,5},{22,6},{23,7},{24,8},{25... | collective-permute-start | bytes 1572872 | tf_op jit(solution)/shard_map/ppermute | solution.py:127
  328.1 0.8 copy-start
  346.6 0.8 copy-start.12
Sparse Core Ops, SparseCore 0:
  9.5 156.7 all-gather.1

commit v2 on v1

v2 whole, which is shorter than its diff:
```python
import functools
import jax
import jax.numpy as jnp
from jax import lax
from jax.experimental import pallas as pl
from jax.experimental.pallas import tpu as pltpu
from jax.sharding import PartitionSpec as P

BLOCKS = 2
GROUP = 32


def sweep_kernel(
    part, block, place, columns, tiles, noise, scale, front, _, out, front_out,
    out_buf, even, odd, out_sem,
):
    steps, rows, depth, size = tiles.shape
    kt = depth // size
    width = front.shape[1]
    group = min(GROUP, rows)
    mine = pl.ds(block * width, width)

    def out_copy(s):
        return pltpu.make_async_copy(out_buf.at[s], out.at[s, mine], out_sem.at[s])

    def one_step(s, source, target):
        def one_group(g, carry):
            picked = [
                jnp.concatenate(
                    [source[columns[(s * rows + g * group + q) * kt + k]] for k in range(kt)], axis=1
                )
                for q in range(group)
            ]
            mixed = [
                jnp.dot(picked[q], tiles[s, g * group + q], preferred_element_type=jnp.float32)
                for q in range(group)
            ]
            for q in range(group):
                r = g * group + q
                lanes = pl.ds(pl.multiple_of(r * size, size), size)
                total = noise[s, mine, lanes].astype(jnp.float32) + mixed[q]
                value = (scale[s, :, lanes] * total).astype(jnp.bfloat16)
                out_buf[s, :, lanes] = value
                target[r] = value
            return carry

        lax.fori_loop(0, rows // group, one_group, 0)
        out_copy(s).start()

    @pl.when(place[0] == part)
    def _active():
        even[...] = front[...]

        def two_steps(i, carry):
            s = steps - 1 - 2 * i
            one_step(s, even, odd)
            one_step(s - 1, odd, even)
            return carry

        lax.fori_loop(0, steps // 2, two_steps, 0)
        front_out[...] = even[...]
        for s in range(steps):
            out_copy(s).wait()


def sweep(place, columns, tiles, noise, scale, front, out, part, block):
    steps = tiles.shape[0]
    width = front.shape[1]
    node_count = noise.shape[-1]
    anywhere = pl.BlockSpec(memory_space=pl.ANY)
    smem = pl.BlockSpec(memory_space=pltpu.SMEM)
    vmem = pl.BlockSpec(memory_space=pltpu.VMEM)
    return pl.pallas_call(
        functools.partial(sweep_kernel, part, block),
        out_shape=(
            jax.ShapeDtypeStruct(out.shape, out.dtype),
            jax.ShapeDtypeStruct(front.shape, front.dtype),
        ),
        in_specs=[smem, smem, vmem, vmem, vmem, vmem, anywhere],
        out_specs=(anywhere, vmem),
        input_output_aliases={6: 0},
        scratch_shapes=[
            pltpu.VMEM((steps, width, node_count), jnp.bfloat16),
            pltpu.VMEM(front.shape, jnp.bfloat16),
            pltpu.VMEM(front.shape, jnp.bfloat16),
            pltpu.SemaphoreType.DMA((steps,)),
        ],
        compiler_params=pltpu.CompilerParams(vmem_limit_bytes=12 << 20),
        name="sweep",
    )(place, columns, tiles, noise, scale, front, out)


def on_device(noise, scale, tiles, columns):
    steps, local_samples, node_count = noise.shape
    local_rows, kt, size = tiles.shape[1:4]
    parts = lax.axis_size("tm")
    place = lax.axis_index("tm").astype(jnp.int32).reshape(1)
    width = local_samples // BLOCKS
    turned = jnp.swapaxes(tiles, 3, 4).reshape(steps, local_rows, kt * size, size)
    full_tiles = lax.all_gather(turned, "space", axis=1, tiled=True)
    full_columns = lax.all_gather(columns, "space", axis=1, tiled=True).reshape(-1)
    scale_rows = scale.reshape(steps, 1, node_count)

    out = jnp.zeros(noise.shape, jnp.bfloat16)
    fronts = [jnp.zeros((node_count // size, width, size), jnp.bfloat16) for _ in range(BLOCKS)]
    for part in reversed(range(parts)):
        for block in range(BLOCKS):
            out, front = sweep(
                place, full_columns, full_tiles, noise, scale_rows, fronts[block], out, part, block
            )
            if part > 0:
                fronts[block] = lax.ppermute(front, "tm", [(part, part - 1)])
    return out


def solution(mesh):
    placed = (
        P("tm", "space", None),
        P("tm", None),
        P("tm", "space", None, None, None),
        P("tm", "space", None),
    )
    return jax.shard_map(
        on_device, mesh=mesh, in_specs=placed, out_specs=P("tm", "space", None), check_vma=False
    )
```

time: 371 us -> 289 us (0.78)
  waiting for transfers between devices: 241 us -> 201 us
  Pallas kernels: 62.6 us -> 24.6 us
    ppermute x14, waiting for transfers between devices: 109 us -> 68.2 us  [on_device(): fronts[block] = lax.ppermute(front, 'tm', [(part, part - 1)])]
    pallas_call x16, Pallas kernels: 62.6 us -> 24.6 us  [sweep(): pl.pallas_call(functools.partial(sweep_kernel, part, block), out_shape=(j...]
    unnamed x31 -> x9, local copies, waits for them, and re-layouts: 11.4 us -> 9.29 us
  transfers between devices with their start and end apart: 15 -> 15, of which waited for: 3 -> 3; matrix products, arithmetic and copies ran while one was open for 0% -> 0% of each run, Pallas kernels for 12% -> 6%
where the time goes in v2:
time: 289 us
  waiting for transfers between devices  201 us (70%)
  Pallas kernels  24.6 us (9%)
  blocking collectives  24.2 us (8%)
  local copies, waits for them, and re-layouts  14.9 us (5%)
  between operations  13.8 us (5%)
  starting transfers between devices  10.9 us (4%)
    all_gather x1, waiting for transfers between devices, on_device(): full_tiles = lax.all_gather(turned, 'space', axis=1, tiled=True)  132 us
    ppermute x14, waiting for transfers between devices, on_device(): fronts[block] = lax.ppermute(front, 'tm', [(part, part - 1)])  68.2 us
    pallas_call x16, Pallas kernels, sweep(): pl.pallas_call(functools.partial(sweep_kernel, part, block), out_shape=(j...  24.6 us
    all_gather x1, blocking collectives, on_device(): lax.all_gather(columns, 'space', axis=1, tiled=True).reshape(-1)  24.2 us
    ppermute x14, starting transfers between devices, on_device(): fronts[block] = lax.ppermute(front, 'tm', [(part, part - 1)])  10.9 us
    unnamed x9, local copies, waits for them, and re-layouts  9.29 us
  transfers between devices with their start and end apart: 15, of which 3 were waited for; matrix products, arithmetic and copies ran while one was open for 0% of the time, Pallas kernels for 6%

profile of v2, /device:TPU:0, one launch (start us, length us, event | category | flops | bytes accessed | tf_op | source)
XLA Modules:
  0.0 289.1 jit_solution(4155800286092535861)
XLA Ops:
  6.5 2.6 copy.26
  9.3 24.2 %all_gather.6 = s32[4,64,3]{2,0,1:T(4,128)S(1)} all-gather(s32[4,4,3]{2,0,1:T(4,128)S(1)} %copy.24), channel_id=1, replica_groups=mesh['tm'=8,'space'=16] {'space'}, dimensions={1}, use_global_device_ids=true | all-gather | bytes 3264 | tf_op jit(solution)/shard_map/all_gather | solution.py:101
  33.8 132.5 %all-gather.2.cloned.1.call-done.tiles = bf16[4,64,384,128]{3,2,1,0:T(8,128)(2,1)} async-done(((bf16[4,4,384,128]{3,2,1,0:T(8,128)(2,1)}), bf16[4,64,384,128]{3,2,1,0:T(8,128)(2,1)}) %all-gather.2.cloned.1.call-update) | async-done | bytes 25165840 | tf_op jit(solution)/shard_map/all_gather | solution.py:100
  166.4 2.6 broadcast_in_dim.3._
  169.0 1.0 copy-done.1
  170.0 8.2 %copy-done = bf16[4,64,384,128]{3,2,1,0:T(8,128)(2,1)S(1)} copy-done((bf16[4,64,384,128]{3,2,1,0:T(8,128)(2,1)S(1)}, bf16[4,64,384,128]{3,2,1,0:T(8,128)(2,1)}, u32[]{:S(2)}) %copy-start) | copy-done | bytes 25165848
  178.8 0.7 collective-permute-start.1
  179.5 0.6 sweep.17
  180.1 0.7 collective-permute-start
  180.9 0.6 sweep.18
  181.5 0.7 collective-permute-start.3
  182.2 0.6 sweep.19
  182.8 0.7 collective-permute-start.2
  183.6 0.6 sweep.20
  184.2 0.7 collective-permute-start.5
  184.9 0.6 sweep.21
  185.5 0.7 collective-permute-start.4
  186.3 0.8 sweep.22
  187.1 0.7 collective-permute-start.7
  187.8 0.6 sweep.23
  188.4 0.7 collective-permute-start.6
  189.1 0.6 sweep.24
  189.8 0.7 collective-permute-start.9
  191.1 0.7 collective-permute-start.8
  192.5 0.7 collective-permute-start.11
  193.8 0.7 collective-permute-start.10
  195.2 1.3 collective-permute-start.13
  196.5 0.9 sweep.29
  197.3 1.3 collective-permute-start.12
  198.6 67.6 %collective-permute-done.13.front = bf16[64,32,128]{2,1,0:T(8,128)(2,1)S(1)} collective-permute-done((bf16[64,32,128]{2,1,0:T(8,128)(2,1)S(1)}, bf16[64,32,128]{2,1,0:T(8,128)(2,1)S(1)}, u32[]{:S(2)}, u32[]{:S(2)}) %collective-permute-start.13) | collective-permute-done | bytes 524320 | tf_op jit(solution)/shard_map/ppermute | solution.py:112
  266.3 7.7 %sweep.30 = (bf16[4,64,8192]{2,1,0:T(8,128)(2,1)}, bf16[64,32,128]{2,1,0:T(8,128)(2,1)}) custom-call(s32[1]{0:T(128)} %bitcast.place, s32[768]{0:T(1024)S(1)} %reshape.13.columns, bf16[4,64,384,128]{3,2,1,0:T(8,128)(2,1)S(1)} %copy-done, bf16[4,64,8192]{2,1,0:T(8,128)(2,1)S(1)} %copy-done.1, ...), custom_call_target="tpu_custom_call", output_to_operand_aliasing={{0}: (6, {})} | custom-call | tf_op jit(solution)/shard_map/sweep/pallas_call | solution.py:73
  274.5 7.7 %sweep.31 = (bf16[4,64,8192]{2,1,0:T(8,128)(2,1)}, bf16[64,32,128]{2,1,0:T(8,128)(2,1)}) custom-call(s32[1]{0:T(128)} %bitcast.place, s32[768]{0:T(1024)S(1)} %reshape.13.columns, bf16[4,64,384,128]{3,2,1,0:T(8,128)(2,1)S(1)} %copy-done, bf16[4,64,8192]{2,1,0:T(8,128)(2,1)S(1)} %copy-done.1, ...), custom_call_target="tpu_custom_call", output_to_operand_aliasing={{0}: (6, {})} | custom-call | tf_op jit(solution)/shard_map/sweep/pallas_call | solution.py:73
  (31 shorter events, 4.2 us)
Async XLA Ops:
  6.5 2.7 copy-start.3
  6.5 27.2 %copy-start.2 = (f32[4,8192]{1,0:T(4,128)S(1)}, f32[4,8192]{1,0:T(4,128)}, u32[]{:S(2)}) copy-start(f32[4,8192]{1,0:T(4,128)} %param.5) | copy-start | bytes 393220
  6.5 159.8 %all-gather.2.cloned.1.call-start = ((), (), s32[]{:S(2)}) async-start(), calls=%async_computation | async-start | bytes 26738688 | tf_op jit(solution)/shard_map/all_gather | solution.py:100
  166.3 3.7 %copy-start.1 = (bf16[4,64,8192]{2,1,0:T(8,128)(2,1)S(1)}, bf16[4,64,8192]{2,1,0:T(8,128)(2,1)}, u32[]{:S(2)}) copy-start(bf16[4,64,8192]{2,1,0:T(8,128)(2,1)} %noise.31) | copy-start | bytes 12582916
  170.0 8.2 %copy-start = (bf16[4,64,384,128]{3,2,1,0:T(8,128)(2,1)S(1)}, bf16[4,64,384,128]{3,2,1,0:T(8,128)(2,1)}, u32[]{:S(2)}) copy-start(bf16[4,64,384,128]{3,2,1,0:T(8,128)(2,1)} %all-gather.2.cloned.1.call-done.tiles) | copy-start | bytes 75497472
  178.8 2.0 collective-permute-start.1
  180.1 2.1 collective-permute-start
  181.5 2.1 collective-permute-start.3
  182.8 2.1 collective-permute-start.2
  184.2 2.1 collective-permute-start.5
  185.5 2.2 collective-permute-start.4
  187.1 2.1 collective-permute-start.7
  188.4 2.1 collective-permute-start.6
  189.8 2.1 collective-permute-start.9
  191.1 2.1 collective-permute-start.8
  192.5 2.1 collective-permute-start.11
  193.8 2.7 collective-permute-start.10
  195.2 71.1 %collective-permute-start.13 = (bf16[64,32,128]{2,1,0:T(8,128)(2,1)S(1)}, bf16[64,32,128]{2,1,0:T(8,128)(2,1)S(1)}, u32[]{:S(2)}, u32[]{:S(2)}) collective-permute-start(bf16[64,32,128]{2,1,0:T(8,128)(2,1)S(1)} %get-tuple-element.61), channel_id=1, source_target_pairs={{16,0},{17,1},{18,2},{19,3},{20,4},{21,5},{22,6},{23,7},{24,8},{25... | collective-permute-start | bytes 1572872 | tf_op jit(solution)/shard_map/ppermute | solution.py:112
  197.3 77.2 %collective-permute-start.12 = (bf16[64,32,128]{2,1,0:T(8,128)(2,1)S(1)}, bf16[64,32,128]{2,1,0:T(8,128)(2,1)S(1)}, u32[]{:S(2)}, u32[]{:S(2)}) collective-permute-start(bf16[64,32,128]{2,1,0:T(8,128)(2,1)S(1)} %get-tuple-element.60), channel_id=1, source_target_pairs={{16,0},{17,1},{18,2},{19,3},{20,4},{21,5},{22,6},{23,7},{24,8},{25... | collective-permute-start | bytes 1572872 | tf_op jit(solution)/shard_map/ppermute | solution.py:112
Sparse Core Ops, SparseCore 0:
  9.5 156.7 all-gather.1
